TPU v7x, 32 devices: a whole 2x2x4 slice. The times are simulated.
32 devices in a mesh: lsec: 4 (over y, x), rsec: 8 (over z, core).
Axes of the slice: x: 2, y: 2, z: 4, core: 2. Of those that a mesh axis runs over, the one named last changes fastest.
Arguments:
- psi: bfloat16 [16, 16, 256, 256], P('lsec', 'rsec'), may hold values from -6 to 6
- left_env: bfloat16 [16, 4, 256, 256], P('lsec'), may hold values from -0.375 to 0.375
- right_env: bfloat16 [16, 4, 256, 256], P('rsec'), may hold values from -0.1875 to 0.1875
- energies: float32 [16, 16], P('lsec', 'rsec'), may hold values from 0.5 to 3
- coef_num: int32 [2], replicated, may hold values from 3 to 9
- coef_den: int32 [2], replicated, may hold values from 4 to 8
Outputs:
- vector_out: bfloat16 [16, 16, 256, 256], P('lsec', 'rsec')
- ritz: float32 [3], replicated
All inputs are finite; a program needn't handle non-finite values.
Results may differ from a plain program's by a relative error of at most 0.015.
Values may be sent and summed in bfloat16 or wider, within the bound.
A program may use at most 64 MiB of HBM per device.

v0:
```python
import functools

import jax
import jax.numpy as jnp
from jax import lax
from jax.experimental import pallas as pl
from jax.experimental.pallas import tpu as pltpu
from jax.sharding import PartitionSpec as P

DIAG = 2
HOPS = 1
TERMS = DIAG + 2 * HOPS
ITERS = 3
eps = 1e-06
SHIFT = 1.75
GRAMS = 16
MESH = pl.DeviceIdType.MESH


def gram_row(i, j):
    return j * (j + 1) // 2 + i


def kernel(
    nl, nr, count,
    psi_hbm, left_hbm, right_hbm, energies, coef_num, coef_den,
    out_hbm, ritz,
    q, stage, left, right, right_t, acc, out_v, local, rows, cols,
    send_sem, recv_sem, in_sem, rsend, rrecv, csend, crecv,
):
    na, nb, size, _ = psi_hbm.shape
    me_l, me_r = lax.axis_index("lsec"), lax.axis_index("rsec")
    has_lo_l, has_hi_l = me_l > 0, me_l < nl - 1
    has_lo_r, has_hi_r = me_r > 0, me_r < nr - 1
    up_dn = jnp.logical_and(has_hi_l, has_lo_r)
    dn_up = jnp.logical_and(has_lo_l, has_hi_r)
    odd = lax.rem(me_l, 2) == 1
    even = jnp.logical_not(odd)
    via_hi = jnp.logical_and(up_dn, jnp.logical_and(odd, me_l + 2 < nl))
    via_lo = jnp.logical_and(dn_up, jnp.logical_and(even, me_l >= 2))
    relay_dn = jnp.logical_and(jnp.logical_and(odd, me_l >= 2), has_lo_r)
    relay_up = jnp.logical_and(jnp.logical_and(even, me_l + 2 < nl), has_hi_r)
    up_up = jnp.logical_and(even, jnp.logical_and(has_hi_l, has_hi_r))
    dn_dn = jnp.logical_and(odd, has_lo_r)

    loads = [
        pltpu.make_async_copy(psi_hbm, q.at[0, 1 : na + 1, 1 : nb + 1], in_sem.at[0]),
        pltpu.make_async_copy(right_hbm, right, in_sem.at[1]),
        pltpu.make_async_copy(left_hbm, left, in_sem.at[2]),
    ]
    for load in loads:
        load.start()

    barrier = pltpu.get_barrier_semaphore()

    def greet(target):
        pl.semaphore_signal(barrier, inc=1, device_id=target, device_id_type=MESH)

    for step in range(1, nr):
        greet((me_l, lax.rem(me_r + step, nr)))
    for step in range(1, nl):
        greet((lax.rem(me_l + step, nl), me_r))

    @pl.when(up_dn)
    def _():
        greet((me_l + 1, me_r - 1))

    @pl.when(dn_up)
    def _():
        greet((me_l - 1, me_r + 1))

    @pl.when(up_up)
    def _():
        greet((me_l + 1, me_r + 1))

    @pl.when(dn_dn)
    def _():
        greet((me_l - 1, me_r - 1))

    def hops(k):
        lo_l, hi_l, lo_r, hi_r = me_l - 1, me_l + 1, me_r - 1, me_r + 1
        here = q.at[k]
        up_ref, dn_ref = here.at[na, 1], here.at[1, nb]
        up_dst, dn_dst = here.at[0, nb + 1], here.at[na + 1, 0]
        up_stage, dn_stage = stage.at[k, 0], stage.at[k, 1]
        no = jnp.logical_not
        return (
            (has_hi_l, has_lo_l, here.at[na, 2 : nb + 1], here.at[0, 2 : nb + 1], (hi_l, me_r), 0, 0),
            (jnp.logical_and(up_dn, no(via_hi)), dn_up, up_ref, up_dst, (hi_l, lo_r), 1, 1),
            (has_lo_l, has_hi_l, here.at[1, 1:nb], here.at[na + 1, 1:nb], (lo_l, me_r), 2, 2),
            (jnp.logical_and(dn_up, no(via_lo)), up_dn, dn_ref, dn_dst, (lo_l, hi_r), 3, 3),
            (has_lo_r, has_hi_r, here.at[2:na, 1], here.at[2:na, nb + 1], (me_l, lo_r), 4, 4),
            (has_hi_r, has_lo_r, here.at[2:na, nb], here.at[2:na, 0], (me_l, hi_r), 5, 5),
            (has_lo_r, has_hi_r, here.at[1, 1], here.at[1, nb + 1], (me_l, lo_r), 6, 6),
            (has_hi_r, has_lo_r, here.at[na, nb], here.at[na, 0], (me_l, hi_r), 7, 7),
            (via_hi, relay_dn, up_ref, up_stage, (me_l + 2, me_r), 1, 8),
            (via_lo, relay_up, dn_ref, dn_stage, (me_l - 2, me_r), 3, 9),
            (relay_dn, None, up_stage, up_dst, (lo_l, lo_r), 8, 1),
            (relay_up, None, dn_stage, dn_dst, (hi_l, hi_r), 9, 3),
        )

    def copy(k, n):
        _, _, src, dst, target, ssem, rsem = hops(k)[n]
        return pltpu.make_async_remote_copy(
            src_ref=src, dst_ref=dst,
            send_sem=send_sem.at[k, ssem], recv_sem=recv_sem.at[k, rsem],
            device_id=target, device_id_type=MESH,
        )

    def send(k, which):
        for n in which:
            pl.when(hops(k)[n][0])(lambda n=n: copy(k, n).start())

    def receive(k, which):
        for n in which:
            pl.when(hops(k)[n][1])(lambda n=n: copy(k, n).wait_recv())

    def forward(k):
        receive(k, (8, 9))
        send(k, (10, 11))

    def clear(missing, slots):
        @pl.when(jnp.logical_not(missing))
        def _():
            for k in range(ITERS):
                for i, j in slots:
                    q[k, i, j] = jnp.zeros((size, size), q.dtype)

    clear(has_lo_l, [(0, j) for j in range(2, nb + 1)])
    clear(dn_up, [(0, nb + 1)])
    clear(has_hi_l, [(na + 1, j) for j in range(1, nb)])
    clear(up_dn, [(na + 1, 0)])
    clear(has_hi_r, [(i, nb + 1) for i in range(1, na)])
    clear(has_lo_r, [(i, 0) for i in range(2, na + 1)])

    local[...] = jnp.zeros(local.shape, jnp.float32)
    partners = nr - 1 + nl - 1
    for other in (up_dn, dn_up, up_up, dn_dn):
        partners = partners + other.astype(jnp.int32)
    loads[0].wait()
    pl.semaphore_wait(barrier, partners)
    send(0, (8, 9, 0, 2, 1, 3, 4, 5, 6, 7))
    loads[1].wait()
    for j in range(nb):
        for t in range(TERMS):
            right_t[j, t] = right[j, t].T
    loads[2].wait()

    def term(i, j, t, source):
        inner = jnp.dot(left[i, t], source, preferred_element_type=jnp.float32)
        return jnp.dot(
            inner.astype(jnp.bfloat16), right_t[j, t], preferred_element_type=jnp.float32
        )

    def gram(i, j, blocks):
        part = jnp.zeros((1, size), jnp.float32)
        for a, b in blocks:
            part += jnp.sum(
                q[i, a + 1, b + 1].astype(jnp.float32) * q[j, a + 1, b + 1].astype(jnp.float32),
                axis=0, keepdims=True,
            )
        row = pl.ds(gram_row(i, j), 1)
        for lane in range(0, size, 128):
            local[row, :] += part[:, lane : lane + 128]

    gram(0, 0, [(a, b) for a in range(na) for b in range(nb)])

    def is_local(t, i, j):
        if t < DIAG:
            return True
        if t < DIAG + HOPS:
            return i >= 1 and j + 1 < nb
        return i + 1 < na and j >= 1

    def offset(t):
        return 0 if t < DIAG else (1 if t < DIAG + HOPS else -1)

    def source_of(k, t, i, j):
        return q[k, i + 1 - offset(t), j + 1 + offset(t)]

    def step(k, carry):
        for i in range(na):
            for j in range(nb):
                own = q[k, i + 1, j + 1]
                total = (energies[j, i] - SHIFT) * own.astype(jnp.float32)
                for t in range(TERMS):
                    if is_local(t, i, j):
                        total += term(i, j, t, source_of(k, t, i, j))
                acc[i, j] = total

        def finish(i, j, ts):
            total = acc[i, j]
            for t in ts:
                total += term(i, j, t, source_of(k, t, i, j))
            acc[i, j] = total
            q[k + 1, i + 1, j + 1] = total.astype(jnp.bfloat16)

        def remote(i, j):
            return [t for t in range(DIAG, TERMS) if not is_local(t, i, j)]

        def grams(blocks):
            lax.fori_loop(0, k + 2, lambda i, c: (gram(i, k + 1, blocks), c)[1], 0)

        def onward(which):
            pl.when(k + 1 < ITERS)(lambda: send(k + 1, which))

        forward(k)
        receive(k, (4, 5, 6, 7))
        for i in range(1, na - 1):
            for j in range(nb):
                finish(i, j, remote(i, j))
        onward((4, 5))
        grams([(i, j) for i in range(1, na - 1) for j in range(nb)])
        receive(k, (0,))
        for j in range(nb - 1):
            finish(0, j, remote(0, j))
        onward((2, 6))
        receive(k, (2,))
        for j in range(1, nb):
            finish(na - 1, j, remote(na - 1, j))
        onward((0, 7))
        grams([(0, j) for j in range(nb - 1)] + [(na - 1, j) for j in range(1, nb)])
        receive(k, (1,))
        finish(0, nb - 1, remote(0, nb - 1))
        onward((9, 3))
        receive(k, (3,))
        finish(na - 1, 0, remote(na - 1, 0))
        onward((8, 1))

        grams([(0, nb - 1), (na - 1, 0)])
        return carry

    lax.fori_loop(0, ITERS, step, 0)

    def spread(slots, me, parts, to, ssem, rsem):
        def copy(n, slot):
            return pltpu.make_async_remote_copy(
                src_ref=slots.at[slot], dst_ref=slots.at[slot],
                send_sem=ssem.at[n], recv_sem=rsem.at[slot],
                device_id=to(lax.rem(me + n, parts)), device_id_type=MESH,
            )

        for n in range(1, parts):
            copy(n, me).start()
        for n in range(1, parts):
            copy(n, lax.rem(me + n, parts)).wait_recv()
        for n in range(1, parts):
            copy(n, me).wait_send()
        total = slots[0]
        for n in range(1, parts):
            total = total + slots[n]
        return total

    totals = jnp.sum(local[...], axis=1, keepdims=True)
    place = lax.broadcasted_iota(jnp.int32, local.shape, 0)
    lanes = lax.broadcasted_iota(jnp.int32, local.shape, 1)
    rows[me_r] = jnp.sum(jnp.where(place == lanes, totals, 0.0), axis=0, keepdims=True)
    cols[me_l] = spread(rows, me_r, nr, lambda r: (me_l, r), rsend, rrecv)
    sums = spread(cols, me_l, nl, lambda l: (l, me_r), csend, crecv)
    sums = sums * count

    def mean(i, j):
        row = gram_row(min(i, j), max(i, j))
        return sums[:, row : row + 1]

    def product(x, y):
        total = jnp.zeros((1, 1), jnp.float32)
        for i in range(ITERS + 1):
            for j in range(ITERS + 1):
                if x[i] is not None and y[j] is not None:
                    total = total + x[i] * y[j] * mean(i, j)
        return total

    def plus(x, y):
        return y if x is None else (x if y is None else x + y)

    def scaled(s, x):
        return [None if part is None else s * part for part in x]

    def combine(*lists):
        return [functools.reduce(plus, parts) for parts in zip(*lists)]

    vec = [lax.rsqrt(mean(0, 0) + eps)] + [None] * ITERS
    previous = [None] * (ITERS + 1)
    for k in range(ITERS):
        sigma = combine([None] + vec[:-1], scaled(SHIFT, vec))
        theta = product(vec, sigma)
        resid = combine(sigma, scaled(-theta, vec))
        if k > 0:
            coef = jnp.full((1, 1), coef_num[k - 1].astype(jnp.float32)) / jnp.full(
                (1, 1), coef_den[k - 1].astype(jnp.float32)
            )
            resid = combine(resid, scaled(-coef, previous))
        ritz[k] = theta[0, 0]
        previous = vec
        vec = scaled(lax.rsqrt(product(resid, resid) + eps), resid)

    stores = []
    for i in range(na):
        for j in range(nb):
            total = acc[i, j] * vec[ITERS]
            for n in range(ITERS):
                total += q[n, i + 1, j + 1].astype(jnp.float32) * vec[n]
            out_v[i, j] = total.astype(jnp.bfloat16)
        stores.append(pltpu.make_async_copy(out_v.at[i], out_hbm.at[i], in_sem.at[i]))
        stores[-1].start()

    for k in range(ITERS):
        for n in range(12):
            pl.when(hops(k)[n][0])(lambda k=k, n=n: copy(k, n).wait_send())
    for store in stores:
        store.wait()


def per_device(nl, nr, psi, left_env, right_env, energies, coef_num, coef_den):
    na, nb, size, _ = psi.shape
    count = 1.0 / float(psi.size * nl * nr)
    anywhere = pl.BlockSpec(memory_space=pl.ANY)
    smem = pl.BlockSpec(memory_space=pltpu.SMEM)
    dma = pltpu.SemaphoreType.DMA
    return pl.pallas_call(
        functools.partial(kernel, nl, nr, count),
        out_shape=(
            jax.ShapeDtypeStruct(psi.shape, jnp.bfloat16),
            jax.ShapeDtypeStruct((ITERS,), jnp.float32),
        ),
        in_specs=[anywhere] * 3 + [smem] * 3,
        out_specs=(anywhere, smem),
        scratch_shapes=[
            pltpu.VMEM((ITERS + 1, na + 2, nb + 2, size, size), jnp.bfloat16),
            pltpu.VMEM((ITERS, 2, size, size), jnp.bfloat16),
            pltpu.VMEM(left_env.shape, jnp.bfloat16),
            pltpu.VMEM(right_env.shape, jnp.bfloat16),
            pltpu.VMEM(right_env.shape, jnp.bfloat16),
            pltpu.VMEM(psi.shape, jnp.float32),
            pltpu.VMEM(psi.shape, jnp.bfloat16),
            pltpu.VMEM((GRAMS, 128), jnp.float32),
            pltpu.VMEM((nr, 1, 128), jnp.float32),
            pltpu.VMEM((nl, 1, 128), jnp.float32),
            dma((ITERS, 10)),
            dma((ITERS, 10)),
            dma((max(3, na),)),
            dma((nr,)),
            dma((nr,)),
            dma((nl,)),
            dma((nl,)),
        ],
        compiler_params=pltpu.CompilerParams(
            collective_id=0, has_side_effects=True, vmem_limit_bytes=60000000
        ),
    )(psi, left_env, right_env, energies.T, coef_num, coef_den)


def solution(mesh):
    in_specs = (
        P("lsec", "rsec", None, None),
        P("lsec", None, None, None),
        P("rsec", None, None, None),
        P("lsec", "rsec"),
        P(),
        P(),
    )
    out_specs = (P("lsec", "rsec", None, None), P())
    body = functools.partial(per_device, mesh.shape["lsec"], mesh.shape["rsec"])
    return jax.shard_map(
        body, mesh=mesh, in_specs=in_specs, out_specs=out_specs, check_vma=False
    )
```

profile of v0, /device:TPU:0, one launch (start us, length us, event | category | flops | bytes accessed | tf_op | source)
XLA Modules:
  0.0 48.8 jit_solution(4128151249848990977)
XLA Ops:
  0.6 45.4 %shard_map.77 = (bf16[4,2,256,256]{3,2,1,0:T(8,128)(2,1)}, f32[3]{0:T(128)}) custom-call(bf16[4,2,256,256]{3,2,1,0:T(8,128)(2,1)} %psi_hbm.1, bf16[4,4,256,256]{3,2,1,0:T(8,128)(2,1)} %left_hbm.1, bf16[2,4,256,256]{3,2,1,0:T(8,128)(2,1)} %right_hbm.1, f32[2,4]{1,0:T(2,128)} %bitcast.1, s32[2]{0:T(128)} %coef_num.1, s32[2]{0:T(128)} %coef_den.1), custom_call_target="tpu_custom_call" | custom-call | tf_op jit(solution)/shard_map/pallas_call | solution.py:321
  46.0 0.0 copy-start
  46.0 2.3 %copy.10 = bf16[4,2,256,256]{3,2,1,0:T(8,128)(2,1)} copy(bf16[4,2,256,256]{3,2,1,0:T(8,128)(2,1)} %get-tuple-element.4) | data formatting | bytes 2097152
  48.3 0.0 copy-done
  48.3 0.5 %copy.11 = f32[3]{0:T(128)} copy(f32[3]{0:T(128)S(1)} %copy-done) | data formatting | bytes 24
Async XLA Ops:
  46.0 2.3 %copy-start = (f32[3]{0:T(128)S(1)}, f32[3]{0:T(128)}, u32[]{:S(2)}) copy-start(f32[3]{0:T(128)} %get-tuple-element.5) | copy-start | bytes 40
where the time goes:
time: 49 us; the launch traced here: 48.8 us
  Pallas kernels  45.4 us (93%)
  local copies, waits for them, and re-layouts  2.78 us (6%)
  between operations  0.65 us (1%)
    pallas_call x1, Pallas kernels, per_device(): pl.pallas_call(functools.partial(kernel, nl, nr, count), out_shape=(jax.S...  45.4 us
    unnamed x4, local copies, waits for them, and re-layouts  2.78 us

commit v1 on v0

v1 whole, which is shorter than its diff:
```python
import functools

import jax
import jax.numpy as jnp
from jax import lax
from jax.experimental import pallas as pl
from jax.experimental.pallas import tpu as pltpu
from jax.sharding import PartitionSpec as P

DIAG = 2
HOPS = 1
TERMS = DIAG + 2 * HOPS
ITERS = 3
eps = 1e-06
SHIFT = 1.75
GRAMS = 16
MESH = pl.DeviceIdType.MESH


def gram_row(i, j):
    return j * (j + 1) // 2 + i


def spans(nr):
    out = []
    while 2 ** len(out) < nr:
        out.append(2 ** len(out))
    return out


def kernel(
    nl, nr, count,
    psi, left_hbm, right_hbm, energies_hbm, num_hbm, den_hbm,
    ahead, prior, scalars,
    energies, coef_num, coef_den, q, stage_up, stage_dn, left, right, right_t, acc, local, early, late,
    in_sem, send_sem, recv_sem, token, esend, erecv, lsend, lrecv,
):
    na, nb, size, _ = psi.shape
    half = size // 2
    parts = nl * nr
    me_l, me_r = lax.axis_index("lsec"), lax.axis_index("rsec")
    me = me_l * nr + me_r
    lo_l, hi_l, lo_r, hi_r = me_l - 1, me_l + 1, me_r - 1, me_r + 1
    both, no = jnp.logical_and, jnp.logical_not
    has_lo_l, has_hi_l = me_l > 0, me_l < nl - 1
    has_lo_r, has_hi_r = me_r > 0, me_r < nr - 1
    up_dn, dn_up = both(has_hi_l, has_lo_r), both(has_lo_l, has_hi_r)
    odd = lax.rem(me_l, 2) == 1
    even = no(odd)
    via_hi = both(up_dn, both(odd, me_l + 2 < nl))
    via_lo = both(even, me_l >= 2)
    relay_up = both(both(odd, me_l >= 2), has_lo_r)
    relay_dn = both(even, me_l + 2 < nl)
    up_up = both(even, both(has_hi_l, has_hi_r))
    dn_dn = both(odd, has_lo_r)

    loads = [
        pltpu.make_async_copy(psi, q.at[0, 1 : na + 1, 1 : nb + 1], in_sem.at[0]),
        pltpu.make_async_copy(right_hbm, right, in_sem.at[1]),
        pltpu.make_async_copy(left_hbm, left, in_sem.at[2]),
    ]
    loads += [
        pltpu.make_async_copy(energies_hbm, energies, in_sem.at[3]),
        pltpu.make_async_copy(num_hbm, coef_num, in_sem.at[4]),
        pltpu.make_async_copy(den_hbm, coef_den, in_sem.at[5]),
    ]
    for load in loads:
        load.start()

    barrier = pltpu.get_barrier_semaphore()

    def greet(l, r):
        pl.semaphore_signal(barrier, inc=1, device_id=(l, r), device_id_type=MESH)

    partners = nl - 1
    for cond, l, r in (
        (has_lo_r, me_l, lo_r), (has_hi_r, me_l, hi_r),
        (up_dn, hi_l, lo_r), (dn_up, lo_l, hi_r),
        (up_up, hi_l, hi_r), (dn_dn, lo_l, lo_r),
    ):
        pl.when(cond)(lambda l=l, r=r: greet(l, r))
        partners = partners + cond.astype(jnp.int32)
    for step in range(1, nl):
        greet(lax.rem(me_l + step, nl), me_r)

    reach = spans(nr)

    def token_send(s):
        d = reach[s]
        for side, cond, r in ((0, me_r + d < nr, me_r + d), (1, me_r >= d, me_r - d)):
            pl.when(cond)(
                lambda side=side, r=r: pl.semaphore_signal(
                    token.at[s, side], inc=1, device_id=(me_l, r), device_id_type=MESH
                )
            )

    def token_wait(s):
        d = reach[s]
        for side, cond in ((0, me_r >= d), (1, me_r + d < nr)):
            pl.when(cond)(lambda side=side: pl.semaphore_wait(token.at[s, side], 1))

    def tokens(s):
        if s < len(reach):
            token_wait(s)
            if s + 1 < len(reach):
                token_send(s + 1)

    RP = 8
    RM = RP + na - 1

    def edges(k):
        here = q.at[k]
        own = psi if k == 0 else here.at[1 : na + 1, 1 : nb + 1]

        def rows(ref, h):
            lead = (slice(None),) * (len(ref.shape) - 2)
            return ref.at[lead + (pl.ds(h * half, half),)]

        out = {
            "U2": (has_hi_l, has_lo_l, own.at[na - 1, 1:nb], here.at[0, 2 : nb + 1], (hi_l, me_r), 0, 0),
            "U1": (both(up_dn, no(via_hi)), dn_up, own.at[na - 1, 0], here.at[0, nb + 1], (hi_l, lo_r), 1, 1),
            "D1": (both(has_lo_l, no(via_lo)), has_hi_l, own.at[0, 0 : nb - 1], here.at[na + 1, 1:nb], (lo_l, me_r), 2, 2),
            "D2": (dn_up, up_dn, own.at[0, nb - 1], here.at[na + 1, 0], (lo_l, hi_r), 3, 3),
        }
        for h in range(2):
            up, dn = rows(stage_up.at[k], h), rows(stage_dn.at[k], h)
            out[f"U1h{h}"] = (via_hi, relay_up, rows(own.at[na - 1, 0], h), up, (me_l + 2, me_r), 4 + h, 4 + h)
            out[f"D1h{h}"] = (via_lo, relay_dn, rows(own.at[0, 0 : nb - 1], h), dn, (me_l - 2, me_r), 6 + h, 6 + h)
            out[f"FU{h}"] = (relay_up, None, up, rows(here.at[0, nb + 1], h), (lo_l, lo_r), RM + na - 1 + h, 1)
            out[f"FD{h}"] = (relay_dn, None, dn, rows(here.at[na + 1, 1:nb], h), (hi_l, me_r), RM + na + 1 + h, 2)
        for i in range(1, na):
            n = RP + i - 1
            out[f"RP{i}"] = (has_lo_r, has_hi_r, own.at[i - 1, 0], here.at[i, nb + 1], (me_l, lo_r), n, n)
            n = RM + i - 1
            out[f"RM{i + 1}"] = (has_hi_r, has_lo_r, own.at[i, nb - 1], here.at[i + 1, 0], (me_l, hi_r), n, n)
        return out

    links = [edges(k) for k in range(ITERS)]

    def copy(k, name):
        _, _, src, dst, target, ssem, rsem = links[k][name]
        return pltpu.make_async_remote_copy(
            src_ref=src, dst_ref=dst,
            send_sem=send_sem.at[k, ssem], recv_sem=recv_sem.at[k, rsem],
            device_id=target, device_id_type=MESH,
        )

    def send(k, *names, when=None):
        if k < ITERS:
            for name in names:
                cond = links[k][name][0]
                cond = cond if when is None else both(cond, when)
                pl.when(cond)(lambda name=name: copy(k, name).start())

    def receive(k, *names, when=None):
        for name in names:
            cond = links[k][name][1]
            cond = cond if when is None else both(cond, when)
            pl.when(cond)(lambda name=name: copy(k, name).wait_recv())

    pl.semaphore_wait(barrier, partners)
    send(0, "U1h0", "D1h0", "U1h1", "D1h1", "U1", when=odd)
    send(0, "D1h0", "D1h1", when=even)
    send(0, "D1", when=odd)
    send(0, "U2", when=even)
    send(0, f"RP{na - 1}", "RM2")
    send(0, "U2", when=odd)
    send(0, "D2", "D1", when=even)
    rest_rp = [f"RP{i}" for i in range(na - 2, 0, -1)]
    rest_rm = [f"RM{i}" for i in range(3, na + 1)]
    send(0, *[name for pair in zip(rest_rp, rest_rm) for name in pair])
    token_send(0) if reach else None

    def clear(missing, slots):
        @pl.when(no(missing))
        def _():
            for k in range(ITERS):
                for i, j in slots:
                    q[k, i, j] = jnp.zeros((size, size), q.dtype)

    clear(has_lo_l, [(0, j) for j in range(2, nb + 1)])
    clear(dn_up, [(0, nb + 1)])
    clear(has_hi_l, [(na + 1, j) for j in range(1, nb)])
    clear(up_dn, [(na + 1, 0)])
    clear(has_hi_r, [(i, nb + 1) for i in range(1, na)])
    clear(has_lo_r, [(i, 0) for i in range(2, na + 1)])
    local[...] = jnp.zeros(local.shape, jnp.float32)

    def row(i):
        return jnp.where(odd, i, na + 1 - i)

    def col(j):
        return jnp.where(odd, j, nb + 1 - j)

    def shift(t):
        return 0 if t < DIAG else (1 if t < DIAG + HOPS else -1)

    def which(t):
        if t < DIAG:
            return t
        other = t + HOPS if t < DIAG + HOPS else t - HOPS
        return jnp.where(odd, t, other)

    def block(k, i, j):
        return q[k, row(i), col(j)]

    def term(k, i, j, t):
        source = block(k, i - shift(t), j + shift(t))
        inner = jnp.dot(left[row(i) - 1, which(t)], source, preferred_element_type=jnp.float32)
        return jnp.dot(
            inner.astype(jnp.bfloat16), right_t[col(j) - 1, which(t)],
            preferred_element_type=jnp.float32,
        )

    def is_local(i, j, t):
        return 1 <= i - shift(t) <= na and 1 <= j + shift(t) <= nb

    every = [(i, j) for i in range(1, na + 1) for j in range(1, nb + 1)]
    last = (1, nb)

    def begin(k, i, j, skip=None):
        total = (energies[col(j) - 1, row(i) - 1] - SHIFT) * block(k, i, j).astype(jnp.float32)
        for t in range(TERMS):
            if is_local(i, j, t) and (i - shift(t), j + shift(t)) != skip:
                total += term(k, i, j, t)
        acc[k % 2, row(i) - 1, col(j) - 1] = total

    def add(x, y, a, b):
        part = jnp.sum(x * y, axis=0, keepdims=True)
        at = pl.ds(gram_row(a, b), 1)
        for lane in range(0, size, 128):
            local[at, :] += part[:, lane : lane + 128]

    def grams(k, blocks):
        for i, j in blocks:
            new = block(k, i, j).astype(jnp.float32)
            for a in range(k + 1):
                add(block(a, i, j).astype(jnp.float32), new, a, k)

    def finish(k, i, j):
        total = acc[k % 2, row(i) - 1, col(j) - 1]
        for t in range(DIAG, TERMS):
            if not is_local(i, j, t):
                total += term(k, i, j, t)
        if k + 1 < ITERS:
            q[k + 1, row(i), col(j)] = total.astype(jnp.bfloat16)
        else:
            acc[k % 2, row(i) - 1, col(j) - 1] = total
            for a in range(ITERS):
                add(block(a, i, j).astype(jnp.float32), total, a, ITERS)
            add(total, total, ITERS, ITERS)

    def everyone(slots, ssem, rsem):
        def to(n):
            at = lax.rem(me + n, parts)
            return pltpu.make_async_remote_copy(
                src_ref=slots.at[me], dst_ref=slots.at[me], send_sem=ssem, recv_sem=rsem,
                device_id=(at // nr, lax.rem(at, nr)), device_id_type=MESH,
            )

        def begin():
            lax.fori_loop(1, parts, lambda n, c: (to(n).start(), c)[1], 0)

        whole = pltpu.make_async_remote_copy(
            src_ref=slots.at[0 : parts - 1], dst_ref=slots.at[0 : parts - 1],
            send_sem=ssem, recv_sem=rsem, device_id=(me_l, me_r), device_id_type=MESH,
        )
        return begin, whole

    def packed(first, size):
        totals = jnp.sum(local[...], axis=1, keepdims=True)
        place = lax.broadcasted_iota(jnp.int32, local.shape, 0)
        lanes = lax.broadcasted_iota(jnp.int32, local.shape, 1)
        return jnp.sum(jnp.where(place == lanes, totals, 0.0), axis=0, keepdims=True)

    early_begin, early_whole = everyone(early, esend, erecv)
    late_begin, late_whole = everyone(late, lsend, lrecv)

    loads[1].wait()
    for j in range(nb):
        for t in range(TERMS):
            right_t[j, t] = right[j, t].T
    for load in loads[:1] + loads[2:]:
        load.wait()
    for i, j in every:
        begin(0, i, j)
    grams(0, every)

    for k in range(ITERS):
        n = k + 1
        for h in range(2):
            receive(k, f"U1h{h}", f"D1h{h}")
            send(k, f"FU{h}", f"FD{h}")
        if k == 0:
            send(0, "D2", when=odd)
            send(0, "U1", when=even)

        receive(k, "U2", "RM2", when=odd)
        receive(k, "D1", f"RP{na - 1}", when=even)
        for j in range(1, nb):
            finish(k, 1, j)
        send(n, "D1", "RP1", when=odd)
        send(n, "U2", f"RM{na}", when=even)

        receive(k, *rest_rp, *rest_rm)
        inner = [(2, nb)] if na > 2 else []
        if na > 2:
            inner.append((na - 1, 1))
        for i, j in inner:
            finish(k, i, j)
        if na > 2:
            send(n, f"RP{na - 1}", "RM2")
        for i in range(2, na):
            for j in range(1, nb + 1):
                if (i, j) not in inner:
                    finish(k, i, j)
        send(n, *[f"RP{i}" for i in range(2, na - 1)], *[f"RM{i}" for i in range(3, na)])
        if k == 1:
            tokens(1)

        receive(k, "D1", f"RP{na - 1}", when=odd)
        receive(k, "U2", "RM2", when=even)
        for j in range(2, nb + 1):
            finish(k, na, j)
        send(n, "U2", f"RM{na}", when=odd)
        send(n, "D1h0", "D1h1", "D1", "RP1", when=even)

        receive(k, "D2", when=odd)
        receive(k, "U1", when=even)
        finish(k, na, 1)
        send(n, "U1h0", "U1h1", "U1", when=odd)
        send(n, "D2", when=even)

        if n < ITERS:
            ready = [b for b in every if b != last]
            for i, j in ready:
                begin(n, i, j, skip=last)
            grams(n, ready)

        receive(k, "U1", when=odd)
        receive(k, "D2", when=even)
        finish(k, *last)
        if n == ITERS - 1:
            for s in range(2, len(reach)):
                tokens(s)
            grams(n, [last])
            early[me] = packed(0, 0)
            early_begin()
        send(n, "D2", when=odd)
        send(n, "U1", when=even)
        if n < ITERS:
            begin(n, *last)
            if nb > 1:
                acc[n % 2, row(2) - 1, col(nb - 1) - 1] += term(n, 2, nb - 1, DIAG)
            if n < ITERS - 1:
                grams(n, [last])
        if k == 0:
            tokens(0)

    late[me] = packed(0, 0)
    late_begin()

    def plus(x, y):
        return y if x is None else (x if y is None else x + y)

    def scaled(s, x):
        return [None if part is None else s * part for part in x]

    def combine(*lists):
        return [functools.reduce(plus, parts) for parts in zip(*lists)]

    def product(x, y):
        total = jnp.zeros((1, 1), jnp.float32)
        for i in range(ITERS):
            for j in range(ITERS):
                if x[i] is not None and y[j] is not None:
                    at = gram_row(min(i, j), max(i, j))
                    total = total + x[i] * y[j] * sums[:, at : at + 1]
        return total

    early_whole.wait_recv()
    sums = jnp.sum(early[...], axis=0) * count
    vec = [lax.rsqrt(sums[:, 0:1] + eps)] + [None] * ITERS
    previous = None
    theta = []
    for k in range(ITERS):
        image = combine([None] + vec[:-1], scaled(SHIFT, vec))
        resid = image
        if k > 0:
            coef = jnp.full((1, 1), coef_num[k - 1].astype(jnp.float32)) / jnp.full(
                (1, 1), coef_den[k - 1].astype(jnp.float32)
            )
            resid = combine(resid, scaled(-coef, previous))
        if k + 1 == ITERS:
            break
        theta.append(product(vec, image))
        resid = combine(resid, scaled(-theta[k], vec))
        previous = vec
        vec = scaled(lax.rsqrt(product(resid, resid) + eps), resid)

    for i in range(na):
        for j in range(nb):
            new = acc[(ITERS - 1) % 2, i, j] * resid[ITERS]
            old = None
            for a in range(ITERS):
                part = q[a, i + 1, j + 1].astype(jnp.float32)
                new += part * resid[a]
                old = plus(old, part * vec[a])
            ahead[i, j] = new
            prior[i, j] = old

    theta_known = product(vec, image)
    both_known = product(resid, vec)
    new_known = product(resid, resid)
    old_known = product(vec, vec)
    early_whole.wait_send()
    for k in range(ITERS):
        for name, link in links[k].items():
            pl.when(link[0])(lambda k=k, name=name: copy(k, name).wait_send())

    late_whole.wait_recv()
    sums = jnp.sum(late[...], axis=0) * count

    def cross(x):
        total = jnp.zeros((1, 1), jnp.float32)
        for a in range(ITERS):
            at = gram_row(a, ITERS)
            total = total + x[a] * sums[:, at : at + 1]
        return total

    at = gram_row(ITERS, ITERS)
    top = resid[ITERS]
    with_vec = top * cross(vec)
    theta.append(theta_known + with_vec)
    overlap = both_known + with_vec
    square = new_known + top * (2.0 * cross(resid) + top * sums[:, at : at + 1])
    norm = square - theta[-1] * (2.0 * overlap - theta[-1] * old_known)
    scale = lax.rsqrt(norm + eps)
    values = [scale, scale * theta[-1]] + theta
    for n, value in enumerate(values):
        scalars[n : n + 1, :] = jnp.broadcast_to(value, (1, scalars.shape[1]))
    late_whole.wait_send()


def close(ahead, prior, scalars, out_hbm, ritz, out_v, sem):
    na, nb = ahead.shape[:2]
    scale, drop = scalars[0:1, 0:1], scalars[1:2, 0:1]
    stores = []
    for i in range(na):
        for j in range(nb):
            out_v[i, j] = (ahead[i, j] * scale - prior[i, j] * drop).astype(jnp.bfloat16)
        stores.append(pltpu.make_async_copy(out_v.at[i], out_hbm.at[i], sem.at[i]))
        stores[-1].start()
    for k in range(ITERS):
        ritz[k] = scalars[2 + k, 0]
    for store in stores:
        store.wait()


def per_device(nl, nr, psi, left_env, right_env, energies, coef_num, coef_den):
    na, nb, size, _ = psi.shape
    count = 1.0 / float(psi.size * nl * nr)
    hbm = pl.BlockSpec(memory_space=pltpu.HBM)
    smem = pl.BlockSpec(memory_space=pltpu.SMEM)
    vmem = pl.BlockSpec(memory_space=pltpu.VMEM)
    dma = pltpu.SemaphoreType.DMA
    flows = 12 + 2 * (na - 1)
    ahead, prior, scalars = pl.pallas_call(
        functools.partial(kernel, nl, nr, count),
        out_shape=(
            pltpu.VMEM(psi.shape, jnp.float32),
            pltpu.VMEM(psi.shape, jnp.float32),
            pltpu.VMEM((8, 128), jnp.float32),
        ),
        in_specs=[hbm] * 6,
        out_specs=(vmem, vmem, vmem),
        scratch_shapes=[
            pltpu.SMEM((nb, na), jnp.float32),
            pltpu.SMEM(coef_num.shape, jnp.int32),
            pltpu.SMEM(coef_den.shape, jnp.int32),
            pltpu.VMEM((ITERS, na + 2, nb + 2, size, size), jnp.bfloat16),
            pltpu.VMEM((ITERS, size, size), jnp.bfloat16),
            pltpu.VMEM((ITERS, nb - 1, size, size), jnp.bfloat16),
            pltpu.VMEM(left_env.shape, jnp.bfloat16),
            pltpu.VMEM(right_env.shape, jnp.bfloat16),
            pltpu.VMEM(right_env.shape, jnp.bfloat16),
            pltpu.VMEM((2,) + psi.shape, jnp.float32),
            pltpu.VMEM((GRAMS, 128), jnp.float32),
            pltpu.VMEM((nl * nr, 1, 128), jnp.float32),
            pltpu.VMEM((nl * nr, 1, 128), jnp.float32),
            dma((6,)),
            dma((ITERS, flows)),
            dma((ITERS, flows)),
            pltpu.SemaphoreType.REGULAR((max(1, len(spans(nr))), 2)),
            dma, dma, dma, dma,
        ],
        compiler_params=pltpu.CompilerParams(
            collective_id=0, has_side_effects=True, vmem_limit_bytes=52000000
        ),
    )(psi, left_env, right_env, energies.T, coef_num, coef_den)
    return pl.pallas_call(
        close,
        out_shape=(
            jax.ShapeDtypeStruct(psi.shape, jnp.bfloat16),
            jax.ShapeDtypeStruct((ITERS,), jnp.float32),
        ),
        in_specs=[vmem] * 3,
        out_specs=(hbm, smem),
        scratch_shapes=[pltpu.VMEM(psi.shape, jnp.bfloat16), dma((na,))],
        compiler_params=pltpu.CompilerParams(vmem_limit_bytes=8000000),
    )(ahead, prior, scalars)


def solution(mesh):
    in_specs = (
        P("lsec", "rsec", None, None),
        P("lsec", None, None, None),
        P("rsec", None, None, None),
        P("lsec", "rsec"),
        P(),
        P(),
    )
    out_specs = (P("lsec", "rsec", None, None), P())
    body = functools.partial(per_device, mesh.shape["lsec"], mesh.shape["rsec"])
    return jax.shard_map(
        body, mesh=mesh, in_specs=in_specs, out_specs=out_specs, check_vma=False
    )
```

time: 49 us -> 44.8 us (0.914)
  Pallas kernels: 45.4 us -> 41.8 us
  local copies, waits for them, and re-layouts: 2.78 us -> 1.98 us
    pallas_call x1 -> x2, Pallas kernels: 45.4 us -> 41.8 us  [the longest x1 40.1 us: per_device(): pl.pallas_call(functools.partial(kernel, nl, nr, count), out_shape=(pltpu...]
    unnamed x4 -> x6, local copies, waits for them, and re-layouts: 2.78 us -> 1.98 us
where the time goes in v1:
time: 44.8 us; the launch traced here: 44.6 us
  Pallas kernels  41.8 us (93%)
  local copies, waits for them, and re-layouts  1.98 us (4%)
  between operations  0.81 us (2%)
    pallas_call x1, Pallas kernels, per_device(): pl.pallas_call(functools.partial(kernel, nl, nr, count), out_shape=(pltpu...  40.1 us
    unnamed x6, local copies, waits for them, and re-layouts  1.98 us
    pallas_call x1, Pallas kernels, per_device(): pl.pallas_call(close, out_shape=(jax.ShapeDtypeStruct(psi.shape, jnp.bflo...  1.73 us

profile of v1, /device:TPU:0, one launch (start us, length us, event | category | flops | bytes accessed | tf_op | source)
XLA Modules:
  0.0 44.6 jit_solution(16769819788494701008)
XLA Ops:
  0.6 0.0 copy-start
  0.6 0.7 %copy-done = f32[4,2]{0,1:T(2,128)S(1)} copy-done((f32[4,2]{0,1:T(2,128)S(1)}, f32[4,2]{0,1:T(2,128)}, u32[]{:S(2)}) %copy-start) | copy-done | bytes 56
  1.3 0.0 copy-start.1
  1.3 0.7 %copy-done.1 = s32[2]{0:T(128)S(1)} copy-done((s32[2]{0:T(128)S(1)}, s32[2]{0:T(128)}, u32[]{:S(2)}) %copy-start.1) | copy-done | bytes 32
  2.0 0.0 copy-start.2
  2.0 0.7 %copy-done.2 = s32[2]{0:T(128)S(1)} copy-done((s32[2]{0:T(128)S(1)}, s32[2]{0:T(128)}, u32[]{:S(2)}) %copy-start.2) | copy-done | bytes 32
  2.6 40.1 %shard_map.77 = (f32[4,2,256,256]{3,2,1,0:T(8,128)S(1)}, f32[4,2,256,256]{3,2,1,0:T(8,128)S(1)}, f32[8,128]{1,0:T(8,128)S(1)}) custom-call(bf16[4,2,256,256]{3,2,1,0:T(8,128)(2,1)} %psi.1, bf16[4,4,256,256]{3,2,1,0:T(8,128)(2,1)} %left_hbm.1, bf16[2,4,256,256]{3,2,1,0:T(8,128)(2,1)} %right_hbm.1, f32[2,4]{1,0:T(2,128)S(1)} %bitcast.1, s32[2]{0:T(128)S(1)} %copy-done.1, ...), custom_call_target="tpu_custom_call" | custom-call | tf_op jit(solution)/shard_map/pallas_call | solution.py:468
  42.7 1.7 %shard_map.78 = (bf16[4,2,256,256]{3,2,1,0:T(8,128)(2,1)}, f32[3]{0:T(128)}) custom-call(f32[4,2,256,256]{3,2,1,0:T(8,128)S(1)} %get-tuple-element.5.ahead, f32[4,2,256,256]{3,2,1,0:T(8,128)S(1)} %get-tuple-element.6.prior, f32[8,128]{1,0:T(8,128)S(1)} %get-tuple-element.7.scalars), custom_call_target="tpu_custom_call" | custom-call | tf_op jit(solution)/shard_map/pallas_call | solution.py:501
Async XLA Ops:
  0.6 0.7 %copy-start = (f32[4,2]{0,1:T(2,128)S(1)}, f32[4,2]{0,1:T(2,128)}, u32[]{:S(2)}) copy-start(f32[4,2]{0,1:T(2,128)} %param.9) | copy-start | bytes 100
  1.3 0.7 %copy-start.1 = (s32[2]{0:T(128)S(1)}, s32[2]{0:T(128)}, u32[]{:S(2)}) copy-start(s32[2]{0:T(128)} %num_hbm.1) | copy-start | bytes 28
  2.0 0.7 %copy-start.2 = (s32[2]{0:T(128)S(1)}, s32[2]{0:T(128)}, u32[]{:S(2)}) copy-start(s32[2]{0:T(128)} %den_hbm.1) | copy-start | bytes 28

commit v2 on v1

--- a/solution.py
+++ b/solution.py
@@ -178,14 +178,6 @@
                 for i, j in slots:
                     q[k, i, j] = jnp.zeros((size, size), q.dtype)
 
-    clear(has_lo_l, [(0, j) for j in range(2, nb + 1)])
-    clear(dn_up, [(0, nb + 1)])
-    clear(has_hi_l, [(na + 1, j) for j in range(1, nb)])
-    clear(up_dn, [(na + 1, 0)])
-    clear(has_hi_r, [(i, nb + 1) for i in range(1, na)])
-    clear(has_lo_r, [(i, 0) for i in range(2, na + 1)])
-    local[...] = jnp.zeros(local.shape, jnp.float32)
-
     def row(i):
         return jnp.where(odd, i, na + 1 - i)
 
@@ -218,9 +210,14 @@
     every = [(i, j) for i in range(1, na + 1) for j in range(1, nb + 1)]
     last = (1, nb)
 
-    def begin(k, i, j, skip=None):
-        total = (energies[col(j) - 1, row(i) - 1] - SHIFT) * block(k, i, j).astype(jnp.float32)
+    def begin(k, i, j, skip=None, only=False, fresh=True):
+        if fresh:
+            total = (energies[col(j) - 1, row(i) - 1] - SHIFT) * block(k, i, j).astype(jnp.float32)
+        else:
+            total = acc[k % 2, row(i) - 1, col(j) - 1]
         for t in range(TERMS):
+            if only and t >= DIAG or not fresh and t < DIAG:
+                continue
             if is_local(i, j, t) and (i - shift(t), j + shift(t)) != skip:
                 total += term(k, i, j, t)
         acc[k % 2, row(i) - 1, col(j) - 1] = total
@@ -276,24 +273,34 @@
     early_begin, early_whole = everyone(early, esend, erecv)
     late_begin, late_whole = everyone(late, lsend, lrecv)
 
+    def forward(k, h):
+        receive(k, f"U1h{h}", f"D1h{h}")
+        send(k, f"FU{h}", f"FD{h}")
+
     loads[1].wait()
     for j in range(nb):
         for t in range(TERMS):
             right_t[j, t] = right[j, t].T
     for load in loads[:1] + loads[2:]:
         load.wait()
-    for i, j in every:
-        begin(0, i, j)
-    grams(0, every)
-
+    forward(0, 0)
+    for j in range(1, nb):
+        begin(0, 1, j)
+    forward(0, 1)
+    send(0, "D2", when=odd)
+    send(0, "U1", when=even)
+    clear(has_lo_l, [(0, j) for j in range(2, nb + 1)])
+    clear(dn_up, [(0, nb + 1)])
+    clear(has_hi_l, [(na + 1, j) for j in range(1, nb)])
+    clear(up_dn, [(na + 1, 0)])
+    clear(has_hi_r, [(i, nb + 1) for i in range(1, na)])
+    clear(has_lo_r, [(i, 0) for i in range(2, na + 1)])
+    local[...] = jnp.zeros(local.shape, jnp.float32)
     for k in range(ITERS):
         n = k + 1
-        for h in range(2):
-            receive(k, f"U1h{h}", f"D1h{h}")
-            send(k, f"FU{h}", f"FD{h}")
-        if k == 0:
-            send(0, "D2", when=odd)
-            send(0, "U1", when=even)
+        if k > 0:
+            for h in range(2):
+                forward(k, h)
 
         receive(k, "U2", "RM2", when=odd)
         receive(k, "D1", f"RP{na - 1}", when=even)
@@ -302,6 +309,10 @@
         send(n, "D1", "RP1", when=odd)
         send(n, "U2", f"RM{na}", when=even)
 
+        if k == 0:
+            for i, j in every:
+                if i > 1 or j == nb:
+                    begin(0, i, j)
         receive(k, *rest_rp, *rest_rm)
         inner = [(2, nb)] if na > 2 else []
         if na > 2:
@@ -317,7 +328,14 @@
         send(n, *[f"RP{i}" for i in range(2, na - 1)], *[f"RM{i}" for i in range(3, na)])
         if k == 1:
             tokens(1)
-
+        if n < ITERS:
+            for i in range(2, na):
+                for j in range(1, nb + 1):
+                    begin(n, i, j, only=True)
+            grams(n, [(i, j) for i in range(1, na) for j in range(1, nb + 1) if (i, j) != last])
+
+        if k == 0:
+            grams(0, every)
         receive(k, "D1", f"RP{na - 1}", when=odd)
         receive(k, "U2", "RM2", when=even)
         for j in range(2, nb + 1):
@@ -332,10 +350,12 @@
         send(n, "D2", when=even)
 
         if n < ITERS:
-            ready = [b for b in every if b != last]
-            for i, j in ready:
-                begin(n, i, j, skip=last)
-            grams(n, ready)
+            for i, j in every:
+                if 1 < i < na:
+                    begin(n, i, j, skip=last, fresh=False)
+                elif (i, j) != last:
+                    begin(n, i, j, skip=last)
+            grams(n, [(na, j) for j in range(1, nb + 1)])
 
         receive(k, "U1", when=odd)
         receive(k, "D2", when=even)
@@ -449,8 +469,8 @@
     for i in range(na):
         for j in range(nb):
             out_v[i, j] = (ahead[i, j] * scale - prior[i, j] * drop).astype(jnp.bfloat16)
-        stores.append(pltpu.make_async_copy(out_v.at[i], out_hbm.at[i], sem.at[i]))
-        stores[-1].start()
+            stores.append(pltpu.make_async_copy(out_v.at[i, j], out_hbm.at[i, j], sem.at[i, j]))
+            stores[-1].start()
     for k in range(ITERS):
         ritz[k] = scalars[2 + k, 0]
     for store in stores:
@@ -495,7 +515,7 @@
             dma, dma, dma, dma,
         ],
         compiler_params=pltpu.CompilerParams(
-            collective_id=0, has_side_effects=True, vmem_limit_bytes=52000000
+            collective_id=0, has_side_effects=True, vmem_limit_bytes=60000000
         ),
     )(psi, left_env, right_env, energies.T, coef_num, coef_den)
     return pl.pallas_call(
@@ -506,7 +526,7 @@
         ),
         in_specs=[vmem] * 3,
         out_specs=(hbm, smem),
-        scratch_shapes=[pltpu.VMEM(psi.shape, jnp.bfloat16), dma((na,))],
+        scratch_shapes=[pltpu.VMEM(psi.shape, jnp.bfloat16), dma((na, nb))],
         compiler_params=pltpu.CompilerParams(vmem_limit_bytes=8000000),
     )(ahead, prior, scalars)
 

time: 44.8 us -> 42.8 us (0.955)
  local copies, waits for them, and re-layouts: 1.98 us -> 0 us
    unnamed x6 -> x0, local copies, waits for them, and re-layouts: 1.98 us -> none
where the time goes in v2:
time: 42.8 us; the launch traced here: 42.7 us
  Pallas kernels  41.9 us (98%)
  between operations  0.8 us (2%)
    pallas_call x1, Pallas kernels, per_device(): pl.pallas_call(functools.partial(kernel, nl, nr, count), out_shape=(pltpu...  40.2 us
    pallas_call x1, Pallas kernels, per_device(): pl.pallas_call(close, out_shape=(jax.ShapeDtypeStruct(psi.shape, jnp.bflo...  1.72 us

profile of v2, /device:TPU:0, one launch (start us, length us, event | category | flops | bytes accessed | tf_op | source)
XLA Modules:
  0.0 42.7 jit_solution(11578580031550543735)
XLA Ops:
  0.6 40.2 %shard_map.77 = (f32[4,2,256,256]{3,2,1,0:T(8,128)S(1)}, f32[4,2,256,256]{3,2,1,0:T(8,128)S(1)}, f32[8,128]{1,0:T(8,128)S(1)}) custom-call(bf16[4,2,256,256]{3,2,1,0:T(8,128)(2,1)} %psi.1, bf16[4,4,256,256]{3,2,1,0:T(8,128)(2,1)} %left_hbm.1, bf16[2,4,256,256]{3,2,1,0:T(8,128)(2,1)} %right_hbm.1, f32[2,4]{1,0:T(2,128)} %bitcast.1, s32[2]{0:T(128)} %num_hbm.1, ...), custom_call_target="tpu_custom_call" | custom-call | tf_op jit(solution)/shard_map/pallas_call | solution.py:488
  40.8 1.7 %shard_map.78 = (bf16[4,2,256,256]{3,2,1,0:T(8,128)(2,1)}, f32[3]{0:T(128)}) custom-call(f32[4,2,256,256]{3,2,1,0:T(8,128)S(1)} %get-tuple-element.5.ahead, f32[4,2,256,256]{3,2,1,0:T(8,128)S(1)} %get-tuple-element.6.prior, f32[8,128]{1,0:T(8,128)S(1)} %get-tuple-element.7.scalars), custom_call_target="tpu_custom_call" | custom-call | tf_op jit(solution)/shard_map/pallas_call | solution.py:521

commit v3 on v2

--- a/solution.py
+++ b/solution.py
@@ -298,9 +298,6 @@
     local[...] = jnp.zeros(local.shape, jnp.float32)
     for k in range(ITERS):
         n = k + 1
-        if k > 0:
-            for h in range(2):
-                forward(k, h)
 
         receive(k, "U2", "RM2", when=odd)
         receive(k, "D1", f"RP{na - 1}", when=even)
@@ -369,6 +366,8 @@
         send(n, "D2", when=odd)
         send(n, "U1", when=even)
         if n < ITERS:
+            for h in range(2):
+                forward(n, h)
             begin(n, *last)
             if nb > 1:
                 acc[n % 2, row(2) - 1, col(nb - 1) - 1] += term(n, 2, nb - 1, DIAG)

time: 42.8 us -> 42.8 us (level)
  no operation moved by 1% of the time
where the time goes in v3:
time: 42.8 us; the launch traced here: 42.7 us
  Pallas kernels  41.9 us (98%)
  between operations  0.8 us (2%)
    pallas_call x1, Pallas kernels, per_device(): pl.pallas_call(functools.partial(kernel, nl, nr, count), out_shape=(pltpu...  40.1 us
    pallas_call x1, Pallas kernels, per_device(): pl.pallas_call(close, out_shape=(jax.ShapeDtypeStruct(psi.shape, jnp.bflo...  1.72 us

profile of v3, /device:TPU:0, one launch (start us, length us, event | category | flops | bytes accessed | tf_op | source)
XLA Modules:
  0.0 42.7 jit_solution(9718921099124704953)
XLA Ops:
  0.6 40.1 %shard_map.77 = (f32[4,2,256,256]{3,2,1,0:T(8,128)S(1)}, f32[4,2,256,256]{3,2,1,0:T(8,128)S(1)}, f32[8,128]{1,0:T(8,128)S(1)}) custom-call(bf16[4,2,256,256]{3,2,1,0:T(8,128)(2,1)} %psi.1, bf16[4,4,256,256]{3,2,1,0:T(8,128)(2,1)} %left_hbm.1, bf16[2,4,256,256]{3,2,1,0:T(8,128)(2,1)} %right_hbm.1, f32[2,4]{1,0:T(2,128)} %bitcast.1, s32[2]{0:T(128)} %num_hbm.1, ...), custom_call_target="tpu_custom_call" | custom-call | tf_op jit(solution)/shard_map/pallas_call | solution.py:487
  40.8 1.7 %shard_map.78 = (bf16[4,2,256,256]{3,2,1,0:T(8,128)(2,1)}, f32[3]{0:T(128)}) custom-call(f32[4,2,256,256]{3,2,1,0:T(8,128)S(1)} %get-tuple-element.5.ahead, f32[4,2,256,256]{3,2,1,0:T(8,128)S(1)} %get-tuple-element.6.prior, f32[8,128]{1,0:T(8,128)S(1)} %get-tuple-element.7.scalars), custom_call_target="tpu_custom_call" | custom-call | tf_op jit(solution)/shard_map/pallas_call | solution.py:520
